TPU v7x, 256 devices: a whole 4x4x8 slice. The times are simulated.
256 devices in a mesh: fsdp: 32 (over z_lo, x, core), seq: 8 (over y, z_hi).
Axes of the slice: x: 4, y: 4, z: 8 (z_hi: 2, z_lo: 4; z = z_hi * 4 + z_lo), core: 2. Of those that a mesh axis runs over, the one named last changes fastest.
Arguments:
- queries: bfloat16 [32768, 3072], P(('fsdp', 'seq')), may hold values from -1000 to 1000
- keys: bfloat16 [32768, 3072], P(('fsdp', 'seq')), may hold values from -1000 to 1000
- values: bfloat16 [32768, 3072], P(('fsdp', 'seq')), may hold values from -6 to 6
- image_ids: int32 [32, 1024], P('fsdp'), may hold values from 0 to 15, never falling along the last dimension, each value on 1 to 512 neighbouring positions
- q_gain: float32 [128], replicated, may hold values from 0.6 to 6
- k_gain: float32 [128], replicated, may hold values from 0.6 to 6
- w_out: bfloat16 [3072, 6144], P('fsdp', 'seq'), may hold values from -0.109375 to 0.109375
- grad_y: bfloat16 [32768, 6144], P('fsdp', 'seq'), may hold values from -6 to 6
Outputs:
- grad_queries: bfloat16 [32768, 24, 128], P('fsdp', 'seq')
- grad_keys: bfloat16 [32768, 24, 128], P('fsdp', 'seq')
- grad_values: bfloat16 [32768, 24, 128], P('fsdp', 'seq')
- grad_w: float32 [3072, 6144], P('fsdp', 'seq')
All inputs are finite; a program needn't handle non-finite values.
Results may differ from a plain program's by a relative error of at most 0.02.
The roundings to bfloat16 on the way count: a program that leaves them out, or rounds other values in their place, can miss the bound.
Values may be sent and summed in bfloat16 or wider, within the bound.
A program may use at most 128 MiB of HBM per device.

v0:
```python
import jax
import jax.numpy as jnp
from jax import lax
from jax.sharding import PartitionSpec as P


def norm_parts(source, gain):
    wide = source.astype(jnp.float32)
    centred = wide - jnp.mean(wide, axis=-1, keepdims=True)
    scale_inv = lax.rsqrt(jnp.mean(centred * centred, axis=-1, keepdims=True) + 1e-06)
    x_hat = centred * scale_inv
    return (x_hat, scale_inv, (x_hat * gain).astype(jnp.bfloat16))


def norm_back(grad_n, x_hat, scale_inv, gain):
    scaled = grad_n * gain
    return scale_inv * (
        scaled
        - jnp.mean(scaled, axis=-1, keepdims=True)
        - x_hat * jnp.mean(scaled * x_hat, axis=-1, keepdims=True)
    )


def probabilities(normalized_queries, normalized_keys, same_image, scale_factor):
    scores = (
        jnp.einsum(
            "krt,irt->rki", normalized_queries, normalized_keys, preferred_element_type=jnp.float32
        )
        * scale_factor
    )
    scores = jnp.where(same_image[None], scores, -1e30)
    row_top = jnp.max(scores, axis=-1, keepdims=True)
    exp_terms = jnp.exp(scores - row_top)
    return exp_terms / jnp.sum(exp_terms, axis=-1, keepdims=True)


def local(queries, keys, values, image_ids, q_gain, k_gain, w_out, grad_y):
    head_dim = q_gain.shape[0]
    tok_rows = queries.shape[0]
    heads_all = queries.shape[1] // head_dim
    scale_factor = head_dim ** (-0.5)
    q_patch = queries.reshape(tok_rows, heads_all, head_dim)
    k_patch = keys.reshape(tok_rows, heads_all, head_dim)
    v_patch = values.reshape(tok_rows, heads_all, head_dim)
    q_local, k_local, value_shard = (
        lax.all_to_all(q_patch, "seq", split_axis=1, concat_axis=0, tiled=True),
        lax.all_to_all(k_patch, "seq", split_axis=1, concat_axis=0, tiled=True),
        lax.all_to_all(v_patch, "seq", split_axis=1, concat_axis=0, tiled=True),
    )
    seq_length = q_local.shape[0]
    local_heads = q_local.shape[1]
    image_row = image_ids[0]
    same_image = image_row[:, None] == image_row[None, :]
    q_hat, q_inv, normalized_queries = norm_parts(q_local, q_gain)
    k_hat, k_inv, normalized_keys = norm_parts(k_local, k_gain)
    prob_rows = probabilities(normalized_queries, normalized_keys, same_image, scale_factor)
    probs_reduced_precision = prob_rows.astype(jnp.bfloat16)
    attended = jnp.einsum(
        "tgi,itp->gtp", probs_reduced_precision, value_shard, preferred_element_type=jnp.float32
    ).astype(jnp.bfloat16)
    attended_flat = attended.reshape(seq_length, local_heads * head_dim)
    partial_g = jnp.einsum(
        "ld,cd->lc",
        grad_y,
        lax.all_gather(w_out, "fsdp", axis=0, tiled=True),
        preferred_element_type=jnp.float32,
    )
    grad_sum = lax.psum_scatter(
        partial_g.astype(jnp.bfloat16), "seq", scatter_dimension=1, tiled=True
    )
    attention_gradient = grad_sum.reshape(seq_length, local_heads, head_dim)
    grad_values = jnp.einsum(
        "jpw,pjy->wjy",
        probs_reduced_precision,
        attention_gradient,
        preferred_element_type=jnp.float32,
    ).astype(jnp.bfloat16)
    probability_gradient = jnp.einsum(
        "krt,irt->rki", attention_gradient, value_shard, preferred_element_type=jnp.float32
    )
    row_delta = jnp.sum(prob_rows * probability_gradient, axis=-1, keepdims=True)
    score_gradient = (prob_rows * (probability_gradient - row_delta) * scale_factor).astype(
        jnp.bfloat16
    )
    normed_query_gradient = jnp.einsum(
        "tgi,itp->gtp", score_gradient, normalized_keys, preferred_element_type=jnp.float32
    )
    normed_key_gradient = jnp.einsum(
        "jpw,pjy->wjy", score_gradient, normalized_queries, preferred_element_type=jnp.float32
    )
    grad_queries = norm_back(normed_query_gradient, q_hat, q_inv, q_gain).astype(jnp.bfloat16)
    grad_keys = norm_back(normed_key_gradient, k_hat, k_inv, k_gain).astype(jnp.bfloat16)
    partial_w = jnp.einsum(
        "lc,ld->cd",
        lax.all_gather(attended_flat, "seq", axis=1, tiled=True),
        grad_y,
        preferred_element_type=jnp.float32,
    )
    summed = lax.psum_scatter(partial_w, "fsdp", scatter_dimension=0, tiled=True)
    grad_w = summed * seq_length ** (-0.5)
    return (grad_queries, grad_keys, grad_values, grad_w)


def solution(mesh):
    in_specs = (
        P(("fsdp", "seq"), None),
        P(("fsdp", "seq"), None),
        P(("fsdp", "seq"), None),
        P("fsdp", None),
        P(),
        P(),
        P("fsdp", "seq"),
        P("fsdp", "seq"),
    )
    out_specs = (
        P("fsdp", "seq", None),
        P("fsdp", "seq", None),
        P("fsdp", "seq", None),
        P("fsdp", "seq"),
    )
    return jax.shard_map(local, mesh=mesh, in_specs=in_specs, out_specs=out_specs, check_vma=False)
```

profile of v0, /device:TPU:8, one launch (start us, length us, event | category | flops | bytes accessed | tf_op | source)
XLA Modules:
  0.0 586.4 jit_solution(3500788171164991081)
XLA Ops:
  7.9 2.4 copy.60
  10.3 11.5 %all-to-all-start = ((bf16[128,24,128]{0,2,1:T(8,128)(2,1)}), bf16[128,24,128]{0,2,1:T(8,128)(2,1)S(1)}, u32[]{:S(2)}, u32[]{:S(2)}) async-start(bf16[128,24,128]{0,2,1:T(8,128)(2,1)} %bitcast), calls=%async_computation | async-start | bytes 1572864 | tf_op jit(solution)/shard_map/all_to_all | solution.py:46
  23.0 23.3 %all-to-all-done = bf16[128,24,128]{0,2,1:T(8,128)(2,1)S(1)} async-done(((bf16[128,24,128]{0,2,1:T(8,128)(2,1)}), bf16[128,24,128]{0,2,1:T(8,128)(2,1)S(1)}, u32[]{:S(2)}, u32[]{:S(2)}) %all-to-all-start) | async-done | bytes 786464 | tf_op jit(solution)/shard_map/all_to_all | solution.py:46
  46.3 6.4 %all-to-all-start.1 = ((bf16[128,24,128]{0,2,1:T(8,128)(2,1)}), bf16[128,24,128]{0,2,1:T(8,128)(2,1)S(1)}, u32[]{:S(2)}, u32[]{:S(2)}) async-start(bf16[128,24,128]{0,2,1:T(8,128)(2,1)} %bitcast.107), calls=%async_computation.1 | async-start | bytes 1572864 | tf_op jit(solution)/shard_map/all_to_all | solution.py:47
  52.7 2.3 copy.69
  55.0 11.3 %all-to-all-done.1 = bf16[128,24,128]{0,2,1:T(8,128)(2,1)S(1)} async-done(((bf16[128,24,128]{0,2,1:T(8,128)(2,1)}), bf16[128,24,128]{0,2,1:T(8,128)(2,1)S(1)}, u32[]{:S(2)}, u32[]{:S(2)}) %all-to-all-start.1) | async-done | bytes 786464 | tf_op jit(solution)/shard_map/all_to_all | solution.py:47
  66.3 7.3 %all-to-all-start.2 = ((bf16[128,24,128]{0,2,1:T(8,128)(2,1)}), bf16[128,24,128]{0,2,1:T(8,128)(2,1)}, u32[]{:S(2)}, u32[]{:S(2)}) async-start(bf16[128,24,128]{0,2,1:T(8,128)(2,1)} %bitcast.106), calls=%async_computation.2 | async-start | bytes 1572864 | tf_op jit(solution)/shard_map/all_to_all | solution.py:48
  80.4 9.0 %all-to-all-done.2 = bf16[128,24,128]{0,2,1:T(8,128)(2,1)} async-done(((bf16[128,24,128]{0,2,1:T(8,128)(2,1)}), bf16[128,24,128]{0,2,1:T(8,128)(2,1)}, u32[]{:S(2)}, u32[]{:S(2)}) %all-to-all-start.2) | async-done | bytes 786464 | tf_op jit(solution)/shard_map/all_to_all | solution.py:48
  89.4 2.3 copy.71
  93.3 2.3 copy-done.3
  99.2 11.0 %fusion.54 = (f32[3,1024]{1,0:T(4,128)S(1)}, f32[3,1024,1024]{1,2,0:T(8,128)}) fusion(pred[1024,1024]{0,1:T(8,128)(4,1)S(1)} %copy-done.12, bf16[1024,3,128]{0,2,1:T(8,128)(2,1)} %get-tuple-element.32, bf16[1024,3,128]{0,2,1:T(8,128)(2,1)} %get-tuple-element.33), kind=kOutput, calls=%fused_computation.65 | convolution fusion | flops 817890304 | bytes 15216640 | tf_op jit(solution)/shard_map/sub | solution.py:33
  110.2 6.6 %fusion.38 = bf16[3,1024,128]{1,2,0:T(8,128)(2,1)} fusion(bf16[1024,3,128]{2,0,1:T(8,128)(2,1)S(1)} %bitcast.104, f32[3,1024,1024]{1,2,0:T(8,128)} %get-tuple-element.29, f32[3,1024]{1,0:T(4,128)S(1)} %get-tuple-element.28), kind=kOutput, calls=%fused_computation.45 | convolution fusion | flops 811991040 | bytes 14168064 | tf_op jit(solution)/shard_map/tgi,itp->gtp/dot_general | solution.py:58
  117.1 9.4 %convolution_convert_fusion = bf16[1024,3072]{1,0:T(8,128)(2,1)} fusion(bf16[1024,768]{1,0:T(8,128)(2,1)S(1)} %copy-done, bf16[3072,768]{1,0:T(8,128)(2,1)} %all-gather.3.cloned.1.call-done), kind=kOutput, calls=%fused_computation.14 | convolution fusion | flops 4834983936 | bytes 12582912 | tf_op jit(solution)/shard_map/ld,cd->lc/dot_general | solution.py:62
  126.5 8.7 %copy.92 = bf16[1024,3072]{0,1:T(8,128)(2,1)} copy(bf16[1024,3072]{1,0:T(8,128)(2,1)} %convolution_convert_fusion) | data formatting | bytes 12582912
  135.2 130.9 %all-gather.5.cloned.1.call-done = bf16[1024,3072]{0,1:T(8,128)(2,1)} async-done(((bf16[1024,384]{0,1:T(8,128)(2,1)}), bf16[1024,3072]{0,1:T(8,128)(2,1)}) %all-gather.5.cloned.1.call-update) | async-done | bytes 6291472 | tf_op jit(solution)/shard_map/all_gather | solution.py:95
  266.1 10.0 %fusion.59 = f32[3072,768]{1,0:T(8,128)} fusion(bf16[1024,3072]{0,1:T(8,128)(2,1)} %all-gather.5.cloned.1.call-done, bf16[1024,768]{1,0:T(8,128)(2,1)S(1)} %copy-done), kind=kOutput, calls=%fused_computation.66 | convolution fusion | flops 4831838208 | bytes 17301504 | tf_op jit(solution)/shard_map/lc,ld->cd/dot_general | solution.py:93
  276.1 143.7 %reduce-scatter.7.cloned.1.call-done = bf16[384,1024]{1,0:T(8,128)(2,1)} async-done(((bf16[3072,1024]{1,0:T(8,128)(2,1)}), bf16[384,1024]{1,0:T(8,128)(2,1)}) %reduce-scatter.7.cloned.1.call-update) | async-done | bytes 786448
  419.8 7.5 %fusion.60 = f32[3,1024,1024]{1,2,0:T(8,128)} fusion(bf16[1024,3,128]{2,0,1:T(8,128)(2,1)S(1)} %bitcast.105, bf16[1024,3,128]{0,2,1:T(8,128)(2,1)} %bitcast.108), kind=kOutput, calls=%fused_computation.67 | convolution fusion | flops 805306368 | bytes 14155776 | tf_op jit(solution)/shard_map/krt,irt->rki/dot_general | solution.py:78
  427.3 19.4 %bitcast_reduce_fusion.1 = (f32[1024,3]{0,1:T(4,128)S(1)}, f32[1024,3]{0,1:T(4,128)S(1)}, f32[3,128,1024]{2,1,0:T(8,128)}) fusion(f32[1024,3]{0,1:T(4,128)S(1)} %rsqrt_bitcast_fusion.1, f32[1024,3]{0,1:T(4,128)S(1)} %get-tuple-element.25, f32[8,3,16,8,128]{4,3,2,1,0:T(8,128)S(1)} %bitcast.102, f32[128]{0:T(128)S(1)} %copy-done.18, ...), kind=kOutput, calls=%fused_computation.33 | convolution fusion | flops 829683712 | bytes 29159936 | tf_op jit(solution)/shard_map/tgi,itp->gtp/dot_general | solution.py:85
  446.7 1.8 fusion.27
  450.3 19.6 %bitcast_reduce_fusion = (f32[1024,3]{0,1:T(4,128)S(1)}, f32[1024,3]{0,1:T(4,128)S(1)}, f32[3,128,1024]{2,1,0:T(8,128)}) fusion(f32[1024,3]{0,1:T(4,128)S(1)} %rsqrt_bitcast_fusion, f32[1024,3]{0,1:T(4,128)S(1)} %get-tuple-element.26, f32[8,3,16,8,128]{4,3,2,1,0:T(8,128)S(1)} %bitcast.99, f32[128]{0:T(128)S(1)} %copy-done.19, ...), kind=kOutput, calls=%fused_computation.26 | convolution fusion | flops 829683712 | bytes 29159936 | tf_op jit(solution)/shard_map/jpw,pjy->wjy/dot_general | solution.py:88
  469.9 1.7 fusion.23
  472.8 7.0 %fusion.43 = bf16[1024,3,128]{0,2,1:T(8,128)(2,1)S(1)} fusion(bf16[1024,3,128]{0,2,1:T(8,128)(2,1)S(1)} %bitcast.109, f32[3,1024,1024]{1,2,0:T(8,128)} %get-tuple-element.29, f32[3,1024]{1,0:T(4,128)S(1)} %get-tuple-element.28), kind=kOutput, calls=%fused_computation.47 | convolution fusion | flops 811991040 | bytes 14168064 | tf_op jit(solution)/shard_map/jpw,pjy->wjy/dot_general | solution.py:72
  481.1 97.2 %reduce-scatter.5.cloned.1.call-done = f32[96,768]{1,0:T(8,128)} async-done(((f32[3072,768]{1,0:T(8,128)}), f32[96,768]{1,0:T(8,128)}) %reduce-scatter.5.cloned.1.call-update) | async-done | bytes 294928 | tf_op jit(solution)/shard_map/reduce_scatter | solution.py:99
  (71 shorter events, 19.7 us)
Async XLA Ops:
  7.2 109.9 %copy-start = (bf16[1024,768]{1,0:T(8,128)(2,1)S(1)}, bf16[1024,768]{1,0:T(8,128)(2,1)}, u32[]{:S(2)}) copy-start(bf16[1024,768]{1,0:T(8,128)(2,1)} %param.15) | copy-start | bytes 4718596
  7.2 109.9 %all-gather.3.cloned.1.call-start = ((), (), s32[]{:S(2)}) async-start(), calls=%async_computation.5 | async-start | bytes 4866048 | tf_op jit(solution)/shard_map/all_gather | solution.py:65
  7.9 13.9 %copy-start.14 = (bf16[128,3072]{1,0:T(8,128)(2,1)S(1)}, bf16[128,3072]{1,0:T(8,128)(2,1)}, u32[]{:S(2)}) copy-start(bf16[128,3072]{1,0:T(8,128)(2,1)} %param.9) | copy-start | bytes 2359300
  10.3 36.0 %all-to-all-start = ((bf16[128,24,128]{0,2,1:T(8,128)(2,1)}), bf16[128,24,128]{0,2,1:T(8,128)(2,1)S(1)}, u32[]{:S(2)}, u32[]{:S(2)}) async-start(bf16[128,24,128]{0,2,1:T(8,128)(2,1)} %bitcast), calls=%async_computation | async-start | bytes 1572864 | tf_op jit(solution)/shard_map/all_to_all | solution.py:46
  46.3 8.7 %copy-start.8 = (bf16[128,24,128]{0,2,1:T(8,128)(2,1)}, bf16[128,24,128]{0,2,1:T(8,128)(2,1)S(1)}, u32[]{:S(2)}) copy-start(bf16[128,24,128]{0,2,1:T(8,128)(2,1)S(1)} %all-to-all-done) | copy-start | bytes 2359300
  46.3 20.0 %all-to-all-start.1 = ((bf16[128,24,128]{0,2,1:T(8,128)(2,1)}), bf16[128,24,128]{0,2,1:T(8,128)(2,1)S(1)}, u32[]{:S(2)}, u32[]{:S(2)}) async-start(bf16[128,24,128]{0,2,1:T(8,128)(2,1)} %bitcast.107), calls=%async_computation.1 | async-start | bytes 1572864 | tf_op jit(solution)/shard_map/all_to_all | solution.py:47
  52.7 21.0 %copy-start.17 = (s32[1,1024]{1,0:T(1,128)S(1)}, s32[1,1024]{1,0:T(1,128)}, u32[]{:S(2)}) copy-start(s32[1,1024]{1,0:T(1,128)} %param.11) | copy-start | bytes 12292
  66.3 7.3 %copy-start.9 = (bf16[128,24,128]{0,2,1:T(8,128)(2,1)}, bf16[128,24,128]{0,2,1:T(8,128)(2,1)S(1)}, u32[]{:S(2)}) copy-start(bf16[128,24,128]{0,2,1:T(8,128)(2,1)S(1)} %all-to-all-done.1) | copy-start | bytes 2359300
  66.3 23.1 %all-to-all-start.2 = ((bf16[128,24,128]{0,2,1:T(8,128)(2,1)}), bf16[128,24,128]{0,2,1:T(8,128)(2,1)}, u32[]{:S(2)}, u32[]{:S(2)}) async-start(bf16[128,24,128]{0,2,1:T(8,128)(2,1)} %bitcast.106), calls=%async_computation.2 | async-start | bytes 1572864 | tf_op jit(solution)/shard_map/all_to_all | solution.py:48
  73.7 192.5 %all-gather.5.cloned.1.call-start = ((), (), s32[]{:S(2)}) async-start(), calls=%async_computation.6 | async-start | bytes 7077888 | tf_op jit(solution)/shard_map/all_gather | solution.py:95
  93.1 4.5 copy-start.6
  93.1 2.5 copy-start.3
  93.3 4.3 copy-start.4
  95.6 1.9 copy-start.18
  95.6 1.9 copy-start.19
  97.6 1.6 copy-start.12
  99.2 11.0 %copy-start.11 = (bf16[8,128,3,128]{3,1,0,2:T(8,128)(2,1)S(1)}, bf16[8,128,3,128]{3,1,0,2:T(8,128)(2,1)}, u32[]{:S(2)}) copy-start(bf16[8,128,3,128]{3,1,0,2:T(8,128)(2,1)} %copy.71) | copy-start | bytes 2359300
  116.8 302.9 %reduce-scatter.7.cloned.1.call-start = ((), (), s32[]{:S(2)}) async-start(), calls=%async_computation.8 | async-start | bytes 7077888
  135.2 443.0 %reduce-scatter.5.cloned.1.call-start = ((), (), s32[]{:S(2)}) async-start(), calls=%async_computation.7 | async-start | bytes 9732096 | tf_op jit(solution)/shard_map/reduce_scatter | solution.py:99
  419.8 7.6 %copy-start.7 = (f32[128,24,128]{0,2,1:T(8,128)S(1)}, f32[128,24,128]{0,2,1:T(8,128)}, u32[]{:S(2)}) copy-start(f32[128,24,128]{0,2,1:T(8,128)} %copy-done.6) | copy-start | bytes 4718596
  419.8 7.6 %copy-start.16 = (bf16[1024,3,128]{0,2,1:T(8,128)(2,1)S(1)}, bf16[1024,3,128]{0,2,1:T(8,128)(2,1)}, u32[]{:S(2)}) copy-start(bf16[1024,3,128]{0,2,1:T(8,128)(2,1)} %get-tuple-element.33) | copy-start | bytes 2359300
  446.7 3.0 copy-start.15
  448.6 1.7 copy-start.5
  472.8 107.1 %copy-start.1 = (bf16[1024,768]{1,0:T(8,128)(2,1)S(1)}, bf16[1024,768]{1,0:T(8,128)(2,1)}, u32[]{:S(2)}) copy-start(bf16[1024,768]{1,0:T(8,128)(2,1)} %param.15) | copy-start | bytes 4718596
  (3 other events, 3.7 us)
Sparse Core Ops, SparseCore 0:
  9.9 106.4 all-gather.2
  119.6 146.5 all-gather.4
  270.3 149.3 reduce-scatter.6
  422.4 155.7 reduce-scatter.4
where the time goes:
time: 587 us; the launch traced here: 586 us
  waiting for transfers between devices  416 us (71%)
  matrix products  90.5 us (15%)
  local copies, waits for them, and re-layouts  27.2 us (5%)
  starting transfers between devices  25.6 us (4%)
  between operations  14 us (2%)
  other arithmetic  13 us (2%)
    unnamed x5, waiting for transfers between devices  144 us
    all_gather x1, waiting for transfers between devices, local(): lax.all_gather(attended_flat, 'seq', axis=1, tiled=True)  131 us
    reduce_scatter x1, waiting for transfers between devices, local(): lax.psum_scatter(partial_w, 'fsdp', scatter_dimension=0, tiled=True)  97.2 us
    all_to_all x1, waiting for transfers between devices, local(): lax.all_to_all(q_patch, 'seq', split_axis=1, concat_axis=0, tiled=True)  23.3 us
    unnamed x47, local copies, waits for them, and re-layouts  22.1 us
    dot_general x1, matrix products, local(): jnp.einsum('jpw,pjy->wjy', score_gradient, normalized_queries, preferred_...  19.6 us
    dot_general x1, matrix products, local(): jnp.einsum('tgi,itp->gtp', score_gradient, normalized_keys, preferred_ele...  19.4 us
  transfers between devices with their start and end apart: 7, of which 6 were waited for; matrix products, arithmetic and copies ran while one was open for 21% of the time, Pallas kernels for 0%

commit v1 on v0

--- a/solution.py
+++ b/solution.py
@@ -35,6 +35,18 @@
 
 
 def local(queries, keys, values, image_ids, q_gain, k_gain, w_out, grad_y):
+
+    def outputs_connect(payload):
+        return jnp.concatenate(
+            jax.lax.all_to_all(
+                jnp.stack(tuple((payload for _ in range(jax.lax.axis_size("seq"))))),
+                axis_name="seq",
+                split_axis=0,
+                concat_axis=0,
+            ),
+            axis=1,
+        )
+
     head_dim = q_gain.shape[0]
     tok_rows = queries.shape[0]
     heads_all = queries.shape[1] // head_dim
@@ -91,10 +103,7 @@
     grad_queries = norm_back(normed_query_gradient, q_hat, q_inv, q_gain).astype(jnp.bfloat16)
     grad_keys = norm_back(normed_key_gradient, k_hat, k_inv, k_gain).astype(jnp.bfloat16)
     partial_w = jnp.einsum(
-        "lc,ld->cd",
-        lax.all_gather(attended_flat, "seq", axis=1, tiled=True),
-        grad_y,
-        preferred_element_type=jnp.float32,
+        "lc,ld->cd", outputs_connect(attended_flat), grad_y, preferred_element_type=jnp.float32
     )
     summed = lax.psum_scatter(partial_w, "fsdp", scatter_dimension=0, tiled=True)
     grad_w = summed * seq_length ** (-0.5)

time: 587 us -> 556 us (0.947)
  waiting for transfers between devices: 416 us -> 168 us
  blocking collectives: 0 us -> 219 us
    all_to_all x0 -> x1, blocking collectives: none -> 219 us  [outputs_connect(): jax.lax.all_to_all(jnp.stack(tuple((payload for _ in range(jax.lax.axis_s...]
    all_gather x1 -> x0, waiting for transfers between devices: 131 us -> none  [local(): lax.all_gather(attended_flat, 'seq', axis=1, tiled=True)]
    unnamed x5 -> x4, waiting for transfers between devices: 144 us -> 20.5 us
    all_gather x1, waiting for transfers between devices: 0.02 us -> 6.71 us  [local(): lax.all_gather(w_out, 'fsdp', axis=0, tiled=True)]
    unnamed x47 -> x43, local copies, waits for them, and re-layouts: 22.1 us -> 23 us
  transfers between devices with their start and end apart: 7 -> 6, of which waited for: 6 -> 6; matrix products, arithmetic and copies ran while one was open for 21% -> 19% of each run, Pallas kernels for 0% -> 0%
where the time goes in v1:
time: 556 us; the launch traced here: 554 us
  blocking collectives  219 us (39%)
  waiting for transfers between devices  168 us (30%)
  matrix products  86.8 us (16%)
  local copies, waits for them, and re-layouts  28.9 us (5%)
  starting transfers between devices  25.5 us (5%)
  between operations  14 us (3%)
  other arithmetic  12.6 us (2%)
    all_to_all x1, blocking collectives, outputs_connect(): jax.lax.all_to_all(jnp.stack(tuple((payload for _ in range(jax.lax.axis_s...  219 us
    reduce_scatter x1, waiting for transfers between devices, local(): lax.psum_scatter(partial_w, 'fsdp', scatter_dimension=0, tiled=True)  96.8 us
    all_to_all x1, waiting for transfers between devices, local(): lax.all_to_all(q_patch, 'seq', split_axis=1, concat_axis=0, tiled=True)  23.3 us
    unnamed x43, local copies, waits for them, and re-layouts  23 us
    unnamed x4, waiting for transfers between devices  20.5 us
    dot_general x1, matrix products, local(): jnp.einsum('tgi,itp->gtp', score_gradient, normalized_keys, preferred_ele...  19.6 us
    dot_general x1, matrix products, local(): jnp.einsum('jpw,pjy->wjy', score_gradient, normalized_queries, preferred_...  19.6 us
    all_to_all x1, starting transfers between devices, local(): lax.all_to_all(q_patch, 'seq', split_axis=1, concat_axis=0, tiled=True)  11.5 us
  transfers between devices with their start and end apart: 6, of which 6 were waited for; matrix products, arithmetic and copies ran while one was open for 19% of the time, Pallas kernels for 0%

profile of v1, /device:TPU:8, one launch (start us, length us, event | category | flops | bytes accessed | tf_op | source)
XLA Modules:
  0.0 554.5 jit_solution(1334746391870315241)
XLA Ops:
  7.9 2.4 copy.61
  10.3 11.5 %all-to-all-start = ((bf16[128,24,128]{0,2,1:T(8,128)(2,1)}), bf16[128,24,128]{0,2,1:T(8,128)(2,1)S(1)}, u32[]{:S(2)}, u32[]{:S(2)}) async-start(bf16[128,24,128]{0,2,1:T(8,128)(2,1)} %bitcast), calls=%async_computation | async-start | bytes 1572864 | tf_op jit(solution)/shard_map/all_to_all | solution.py:58
  23.0 23.3 %all-to-all-done = bf16[128,24,128]{0,2,1:T(8,128)(2,1)S(1)} async-done(((bf16[128,24,128]{0,2,1:T(8,128)(2,1)}), bf16[128,24,128]{0,2,1:T(8,128)(2,1)S(1)}, u32[]{:S(2)}, u32[]{:S(2)}) %all-to-all-start) | async-done | bytes 786464 | tf_op jit(solution)/shard_map/all_to_all | solution.py:58
  46.3 6.4 %all-to-all-start.1 = ((bf16[128,24,128]{0,2,1:T(8,128)(2,1)}), bf16[128,24,128]{0,2,1:T(8,128)(2,1)S(1)}, u32[]{:S(2)}, u32[]{:S(2)}) async-start(bf16[128,24,128]{0,2,1:T(8,128)(2,1)} %bitcast.111), calls=%async_computation.1 | async-start | bytes 1572864 | tf_op jit(solution)/shard_map/all_to_all | solution.py:59
  52.7 2.3 copy.70
  55.0 11.3 %all-to-all-done.1 = bf16[128,24,128]{0,2,1:T(8,128)(2,1)S(1)} async-done(((bf16[128,24,128]{0,2,1:T(8,128)(2,1)}), bf16[128,24,128]{0,2,1:T(8,128)(2,1)S(1)}, u32[]{:S(2)}, u32[]{:S(2)}) %all-to-all-start.1) | async-done | bytes 786464 | tf_op jit(solution)/shard_map/all_to_all | solution.py:59
  66.3 7.3 %all-to-all-start.2 = ((bf16[128,24,128]{0,2,1:T(8,128)(2,1)}), bf16[128,24,128]{0,2,1:T(8,128)(2,1)}, u32[]{:S(2)}, u32[]{:S(2)}) async-start(bf16[128,24,128]{0,2,1:T(8,128)(2,1)} %bitcast.110), calls=%async_computation.2 | async-start | bytes 1572864 | tf_op jit(solution)/shard_map/all_to_all | solution.py:60
  80.3 9.1 %all-to-all-done.2 = bf16[128,24,128]{0,2,1:T(8,128)(2,1)} async-done(((bf16[128,24,128]{0,2,1:T(8,128)(2,1)}), bf16[128,24,128]{0,2,1:T(8,128)(2,1)}, u32[]{:S(2)}, u32[]{:S(2)}) %all-to-all-start.2) | async-done | bytes 786464 | tf_op jit(solution)/shard_map/all_to_all | solution.py:60
  89.4 2.3 copy.72
  93.3 2.3 copy-done.3
  99.0 10.7 %fusion.54 = (f32[3,1024]{1,0:T(4,128)S(1)}, f32[3,1024,1024]{1,2,0:T(8,128)}) fusion(pred[1024,1024]{0,1:T(8,128)(4,1)S(1)} %copy-done.12, bf16[1024,3,128]{0,2,1:T(8,128)(2,1)S(1)} %get-tuple-element.32, bf16[1024,3,128]{0,2,1:T(8,128)(2,1)} %get-tuple-element.33), kind=kOutput, calls=%fused_computation.65 | convolution fusion | flops 817890304 | bytes 15216640 | tf_op jit(solution)/shard_map/sub | solution.py:33
  109.7 6.7 %all-gather.2.cloned.1.call-done = bf16[3072,768]{1,0:T(8,128)(2,1)} async-done(((bf16[96,768]{1,0:T(8,128)(2,1)}), bf16[3072,768]{1,0:T(8,128)(2,1)}) %all-gather.2.cloned.1.call-update) | async-done | bytes 4718608 | tf_op jit(solution)/shard_map/all_gather | solution.py:77
  116.4 9.3 %convolution_convert_fusion = bf16[1024,3072]{1,0:T(8,128)(2,1)} fusion(bf16[1024,768]{1,0:T(8,128)(2,1)S(1)} %copy-done, bf16[3072,768]{1,0:T(8,128)(2,1)} %all-gather.2.cloned.1.call-done), kind=kOutput, calls=%fused_computation.14 | convolution fusion | flops 4834983936 | bytes 12582912 | tf_op jit(solution)/shard_map/ld,cd->lc/dot_general | solution.py:74
  125.7 8.7 %copy.93 = bf16[1024,3072]{0,1:T(8,128)(2,1)} copy(bf16[1024,3072]{1,0:T(8,128)(2,1)} %convolution_convert_fusion) | data formatting | bytes 12582912
  135.5 5.7 %fusion.38 = bf16[3,1024,128]{1,2,0:T(8,128)(2,1)S(1)} fusion(bf16[1024,3,128]{2,0,1:T(8,128)(2,1)S(1)} %bitcast.108, f32[3,1024,1024]{1,2,0:T(8,128)} %get-tuple-element.29, f32[3,1024]{1,0:T(4,128)S(1)} %get-tuple-element.28), kind=kOutput, calls=%fused_computation.45 | convolution fusion | flops 811991040 | bytes 14168064 | tf_op jit(solution)/shard_map/tgi,itp->gtp/dot_general | solution.py:70
  142.0 218.8 %all_to_all.41 = bf16[8,1024,384]{1,2,0:T(8,128)(2,1)S(1)} all-to-all(bf16[8,1024,384]{1,2,0:T(8,128)(2,1)S(1)} %stack.3), channel_id=1, replica_groups=mesh['fsdp'=32,'seq'=8] {'seq'}, dimensions={0} | all-to-all | bytes 12582912 | tf_op jit(solution)/shard_map/all_to_all | solution.py:41
  360.8 7.4 %fusion.59 = f32[3072,768]{1,0:T(8,128)} fusion(bf16[1024,3072]{0,1:T(8,128)(2,1)S(1)} %bitcast.107, bf16[1024,768]{1,0:T(8,128)(2,1)S(1)} %copy-done), kind=kOutput, calls=%fused_computation.66 | convolution fusion | flops 4831838208 | bytes 17301504 | tf_op jit(solution)/shard_map/lc,ld->cd/dot_general | solution.py:105
  368.2 19.8 %reduce-scatter.7.cloned.1.call-done = bf16[384,1024]{1,0:T(8,128)(2,1)} async-done(((bf16[3072,1024]{1,0:T(8,128)(2,1)}), bf16[384,1024]{1,0:T(8,128)(2,1)}) %reduce-scatter.7.cloned.1.call-update) | async-done | bytes 786448
  388.0 7.5 %fusion.60 = f32[3,1024,1024]{1,2,0:T(8,128)} fusion(bf16[1024,3,128]{2,0,1:T(8,128)(2,1)S(1)} %bitcast.109, bf16[1024,3,128]{0,2,1:T(8,128)(2,1)} %bitcast.112), kind=kOutput, calls=%fused_computation.67 | convolution fusion | flops 805306368 | bytes 14155776 | tf_op jit(solution)/shard_map/krt,irt->rki/dot_general | solution.py:90
  395.5 19.6 %bitcast_reduce_fusion.1 = (f32[1024,3]{0,1:T(4,128)S(1)}, f32[1024,3]{0,1:T(4,128)S(1)}, f32[3,128,1024]{2,1,0:T(8,128)}) fusion(f32[1024,3]{0,1:T(4,128)S(1)} %rsqrt_bitcast_fusion.1, f32[1024,3]{0,1:T(4,128)S(1)} %get-tuple-element.25, f32[8,3,16,8,128]{4,3,2,1,0:T(8,128)S(1)} %bitcast.105, f32[128]{0:T(128)S(1)} %copy-done.16, ...), kind=kOutput, calls=%fused_computation.33 | convolution fusion | flops 829683712 | bytes 29159936 | tf_op jit(solution)/shard_map/tgi,itp->gtp/dot_general | solution.py:97
  415.2 1.8 fusion.27
  418.7 19.6 %bitcast_reduce_fusion = (f32[1024,3]{0,1:T(4,128)S(1)}, f32[1024,3]{0,1:T(4,128)S(1)}, f32[3,128,1024]{2,1,0:T(8,128)}) fusion(f32[1024,3]{0,1:T(4,128)S(1)} %rsqrt_bitcast_fusion, f32[1024,3]{0,1:T(4,128)S(1)} %get-tuple-element.26, f32[8,3,16,8,128]{4,3,2,1,0:T(8,128)S(1)} %bitcast.102, f32[128]{0:T(128)S(1)} %copy-done.17, ...), kind=kOutput, calls=%fused_computation.26 | convolution fusion | flops 829683712 | bytes 29159936 | tf_op jit(solution)/shard_map/jpw,pjy->wjy/dot_general | solution.py:100
  441.2 7.1 %fusion.43 = bf16[1024,3,128]{0,2,1:T(8,128)(2,1)S(1)} fusion(bf16[1024,3,128]{0,2,1:T(8,128)(2,1)S(1)} %bitcast.113, f32[3,1024,1024]{1,2,0:T(8,128)} %get-tuple-element.29, f32[3,1024]{1,0:T(4,128)S(1)} %get-tuple-element.28), kind=kOutput, calls=%fused_computation.47 | convolution fusion | flops 811991040 | bytes 14168064 | tf_op jit(solution)/shard_map/jpw,pjy->wjy/dot_general | solution.py:84
  449.4 96.8 %reduce-scatter.5.cloned.1.call-done = f32[96,768]{1,0:T(8,128)} async-done(((f32[3072,768]{1,0:T(8,128)}), f32[96,768]{1,0:T(8,128)}) %reduce-scatter.5.cloned.1.call-update) | async-done | bytes 294928 | tf_op jit(solution)/shard_map/reduce_scatter | solution.py:108
  (66 shorter events, 22.7 us)
Async XLA Ops:
  7.2 109.2 %copy-start = (bf16[1024,768]{1,0:T(8,128)(2,1)S(1)}, bf16[1024,768]{1,0:T(8,128)(2,1)}, u32[]{:S(2)}) copy-start(bf16[1024,768]{1,0:T(8,128)(2,1)} %param.15) | copy-start | bytes 4718596
  7.2 109.2 %all-gather.2.cloned.1.call-start = ((), (), s32[]{:S(2)}) async-start(), calls=%async_computation.6 | async-start | bytes 4866048 | tf_op jit(solution)/shard_map/all_gather | solution.py:77
  7.9 13.9 %copy-start.14 = (bf16[128,3072]{1,0:T(8,128)(2,1)S(1)}, bf16[128,3072]{1,0:T(8,128)(2,1)}, u32[]{:S(2)}) copy-start(bf16[128,3072]{1,0:T(8,128)(2,1)} %param.9) | copy-start | bytes 2359300
  10.3 36.0 %all-to-all-start = ((bf16[128,24,128]{0,2,1:T(8,128)(2,1)}), bf16[128,24,128]{0,2,1:T(8,128)(2,1)S(1)}, u32[]{:S(2)}, u32[]{:S(2)}) async-start(bf16[128,24,128]{0,2,1:T(8,128)(2,1)} %bitcast), calls=%async_computation | async-start | bytes 1572864 | tf_op jit(solution)/shard_map/all_to_all | solution.py:58
  46.3 8.7 %copy-start.8 = (bf16[128,24,128]{0,2,1:T(8,128)(2,1)}, bf16[128,24,128]{0,2,1:T(8,128)(2,1)S(1)}, u32[]{:S(2)}) copy-start(bf16[128,24,128]{0,2,1:T(8,128)(2,1)S(1)} %all-to-all-done) | copy-start | bytes 2359300
  46.3 20.0 %all-to-all-start.1 = ((bf16[128,24,128]{0,2,1:T(8,128)(2,1)}), bf16[128,24,128]{0,2,1:T(8,128)(2,1)S(1)}, u32[]{:S(2)}, u32[]{:S(2)}) async-start(bf16[128,24,128]{0,2,1:T(8,128)(2,1)} %bitcast.111), calls=%async_computation.1 | async-start | bytes 1572864 | tf_op jit(solution)/shard_map/all_to_all | solution.py:59
  52.7 21.0 %copy-start.15 = (s32[1,1024]{1,0:T(1,128)S(1)}, s32[1,1024]{1,0:T(1,128)}, u32[]{:S(2)}) copy-start(s32[1,1024]{1,0:T(1,128)} %param.11) | copy-start | bytes 12292
  66.3 7.3 %copy-start.9 = (bf16[128,24,128]{0,2,1:T(8,128)(2,1)}, bf16[128,24,128]{0,2,1:T(8,128)(2,1)S(1)}, u32[]{:S(2)}) copy-start(bf16[128,24,128]{0,2,1:T(8,128)(2,1)S(1)} %all-to-all-done.1) | copy-start | bytes 2359300
  66.3 23.1 %all-to-all-start.2 = ((bf16[128,24,128]{0,2,1:T(8,128)(2,1)}), bf16[128,24,128]{0,2,1:T(8,128)(2,1)}, u32[]{:S(2)}, u32[]{:S(2)}) async-start(bf16[128,24,128]{0,2,1:T(8,128)(2,1)} %bitcast.110), calls=%async_computation.2 | async-start | bytes 1572864 | tf_op jit(solution)/shard_map/all_to_all | solution.py:60
  73.7 314.4 %reduce-scatter.7.cloned.1.call-start = ((), (), s32[]{:S(2)}) async-start(), calls=%async_computation.8 | async-start | bytes 7077888
  76.7 1.2 copy-start.2
  91.7 1.4 copy-start.10
  93.1 4.5 copy-start.6
  93.1 2.5 copy-start.3
  93.3 4.3 copy-start.4
  95.6 1.9 copy-start.16
  95.6 1.9 copy-start.17
  97.6 1.4 copy-start.12
  134.4 1.1 copy-start.11
  134.4 411.8 %reduce-scatter.5.cloned.1.call-start = ((), (), s32[]{:S(2)}) async-start(), calls=%async_computation.7 | async-start | bytes 9732096 | tf_op jit(solution)/shard_map/reduce_scatter | solution.py:108
  388.0 7.5 %copy-start.7 = (f32[128,24,128]{0,2,1:T(8,128)S(1)}, f32[128,24,128]{0,2,1:T(8,128)}, u32[]{:S(2)}) copy-start(f32[128,24,128]{0,2,1:T(8,128)} %copy-done.6) | copy-start | bytes 4718596
  417.0 1.7 copy-start.5
  440.1 1.2 copy-start.13
  441.2 106.7 %copy-start.1 = (bf16[1024,768]{1,0:T(8,128)(2,1)S(1)}, bf16[1024,768]{1,0:T(8,128)(2,1)}, u32[]{:S(2)}) copy-start(bf16[1024,768]{1,0:T(8,128)(2,1)} %param.15) | copy-start | bytes 4718596
Sparse Core Ops, SparseCore 0:
  9.9 106.4 all-gather.1
  134.5 253.4 reduce-scatter.6
  390.8 155.4 reduce-scatter.4
